TPU v7x, 32 devices: a whole 2x2x4 slice. The times are simulated.
32 devices in a mesh: fsdp: 8 (over y, x, core), ulysses: 4 (over z).
Axes of the slice: x: 2, y: 2, z: 4, core: 2. Of those that a mesh axis runs over, the one named last changes fastest.
Arguments:
- layer_input: bfloat16 [24, 1024, 2048], P('fsdp', 'ulysses'), may hold values from -6 to 6
- cotangent: bfloat16 [24, 1024, 2048], P('fsdp', 'ulysses'), may hold values from -6 to 6
- positions: int32 [24, 1024], P('fsdp', 'ulysses'), may hold values from 0 to 4095
- block_ids: int32 [24, 1024], P('fsdp'), may hold values from 0 to 7, never falling along the last dimension, each value on 1 to 256 neighbouring positions
- skip_mask: int32 [24], P('fsdp'), may hold values 0 or 1
- attn_gain: bfloat16 [2048], P('fsdp'), may hold values from 0.5 to 1.5
- w_query: bfloat16 [2048, 2048], P('fsdp'), may hold values from -0.125 to 0.125
- w_key: bfloat16 [2048, 512], P('fsdp'), may hold values from -0.125 to 0.125
- w_value: bfloat16 [2048, 512], P('fsdp'), may hold values from -0.125 to 0.125
- w_out: bfloat16 [2048, 2048], P('fsdp'), may hold values from -1 to 1
- mlp_gain: bfloat16 [2048], P('fsdp'), may hold values from 0.5 to 1.5
- w_gate: bfloat16 [2048, 5632], P('fsdp'), may hold values from -0.125 to 0.125
- w_up: bfloat16 [2048, 5632], P('fsdp'), may hold values from -0.125 to 0.125
- w_down: bfloat16 [5632, 2048], P(None, 'fsdp'), may hold values from -0.078125 to 0.078125
Outputs:
- output: bfloat16 [24, 1024, 2048], P('fsdp', 'ulysses')
- grad_input: bfloat16 [24, 1024, 2048], P('fsdp', 'ulysses')
- grad_attn_gain: float32 [2048], P('fsdp')
- grad_w_query: float32 [2048, 2048], P('fsdp')
- grad_w_key: float32 [2048, 512], P('fsdp')
- grad_w_value: float32 [2048, 512], P('fsdp')
- grad_w_out: float32 [2048, 2048], P('fsdp')
- grad_mlp_gain: float32 [2048], P('fsdp')
- grad_w_gate: float32 [2048, 5632], P('fsdp')
- grad_w_up: float32 [2048, 5632], P('fsdp')
- grad_w_down: float32 [5632, 2048], P(None, 'fsdp')
Inputs may be any that keep to these rules, and one draw needn't show every extreme that they name: `block_ids`: within a sequence block numbers never fall, every number of 0 to 7 occurs, and a block has 1 to 256 tokens.
All inputs are finite; a program needn't handle non-finite values. No bound on the sum of `skip_mask` on one device may be relied on, other than what follows from the above.
Results may differ from a plain program's by a relative error of at most 0.022.
Values may be sent and summed in bfloat16 or wider, within the bound.
No kernel may reach another device: no remote copies, remote signals or barrier semaphores. Data moves between devices by JAX's collectives and lax.ppermute only.
A program may use at most 640 MiB of HBM per device.

v0:
```python
import math
import jax
import jax.numpy as jnp
from jax import lax
from jax.sharding import PartitionSpec as P

H = 16
KVH = 4
HD = 128
epsilon = 1e-05


def rotary_tables(token_positions, head_size):
    half_size = head_size // 2
    frequency = jnp.exp(
        jnp.arange(half_size, dtype=jnp.float32) * (-2.0 * math.log(10000.0) / head_size)
    )
    angles = token_positions.astype(jnp.float32)[..., None] * frequency
    cosine = jnp.concatenate([jnp.cos(angles), jnp.cos(angles)], -1)
    sine_table = jnp.concatenate([jnp.sin(angles), jnp.sin(angles)], -1)
    return (cosine, sine_table)


def rotate(values, cosine, sine_table):
    half_size = values.shape[-1] // 2
    turned = jnp.concatenate([-values[..., half_size:], values[..., :half_size]], -1)
    return values * cosine[..., None, :] + turned * sine_table[..., None, :]


def unrotate(gradients, cosine, sine_table):
    half_size = gradients.shape[-1] // 2
    scaled = gradients * sine_table[..., None, :]
    turned = jnp.concatenate([scaled[..., half_size:], -scaled[..., :half_size]], -1)
    return gradients * cosine[..., None, :] + turned


def on_device(
    layer_input,
    cotangent,
    positions,
    block_ids,
    skip_mask,
    attn_gain,
    w_query,
    w_key,
    w_value,
    w_out,
    mlp_gain,
    w_gate,
    w_up,
    w_down,
):
    seq_count, local_len, width = layer_input.shape
    row_total = seq_count * local_len
    fsdp_size = lax.axis_size("fsdp")
    ulysses_size = lax.axis_size("ulysses")
    repeat_count = max(1, ulysses_size // KVH)
    head_scale = 1.0 / math.sqrt(HD)
    query_width = H * HD
    pair_width = KVH * HD
    hidden_width = w_gate.shape[1]
    gain_one, query_full, key_full, value_full, out_full = (
        lax.all_gather(attn_gain, "fsdp", axis=0, tiled=True),
        lax.all_gather(w_query, "fsdp", axis=0, tiled=True),
        lax.all_gather(w_key, "fsdp", axis=0, tiled=True),
        lax.all_gather(w_value, "fsdp", axis=0, tiled=True),
        lax.all_gather(w_out, "fsdp", axis=0, tiled=True),
    )
    keep_rows = jnp.repeat((1 - skip_mask).astype(jnp.float32), local_len)[:, None]
    inputs_flat = layer_input.astype(jnp.float32).reshape(row_total, width)
    inv_one = lax.rsqrt(jnp.mean(inputs_flat * inputs_flat, -1, keepdims=True) + epsilon)
    unit_one = inputs_flat * inv_one
    normed_one = (unit_one * gain_one.astype(jnp.float32)).astype(jnp.bfloat16)
    query_pre = jnp.dot(normed_one, query_full, preferred_element_type=jnp.float32).reshape(
        seq_count, local_len, H, HD
    )
    key_pre = jnp.dot(normed_one, key_full, preferred_element_type=jnp.float32).reshape(
        seq_count, local_len, KVH, HD
    )
    value_pre = jnp.dot(normed_one, value_full, preferred_element_type=jnp.float32).reshape(
        seq_count, local_len, KVH, HD
    )
    cosine, sine_table = rotary_tables(positions, HD)
    query_sent = rotate(query_pre, cosine, sine_table).astype(jnp.bfloat16)
    key_sent = jnp.repeat(rotate(key_pre, cosine, sine_table), repeat_count, axis=2).astype(
        jnp.bfloat16
    )
    value_sent = jnp.repeat(value_pre, repeat_count, axis=2).astype(jnp.bfloat16)
    query_heads, key_heads, value_heads = (
        lax.all_to_all(query_sent, "ulysses", split_axis=2, concat_axis=1, tiled=True),
        lax.all_to_all(key_sent, "ulysses", split_axis=2, concat_axis=1, tiled=True),
        lax.all_to_all(value_sent, "ulysses", split_axis=2, concat_axis=1, tiled=True),
    )
    full_len = query_heads.shape[1]
    local_heads = query_heads.shape[2]
    local_slots = key_heads.shape[2]
    group_size = local_heads // local_slots

    def scores_for(query_seq, key_seq, block_row):
        grouped = query_seq.reshape(full_len, local_slots, group_size, HD)
        raw_scores = (
            jnp.einsum("qsgd,ksd->sgqk", grouped, key_seq, preferred_element_type=jnp.float32)
            * head_scale
        )
        allowed = block_row[None, :] <= block_row[:, None]
        return jnp.where(allowed, raw_scores, -1e30)

    def attend(record):
        query_seq, key_seq, value_seq, block_row = record
        scores = scores_for(query_seq, key_seq, block_row)
        largest = jnp.max(scores, -1, keepdims=True)
        exponent = jnp.exp(scores - largest)
        row_sums = jnp.sum(exponent, -1, keepdims=True)
        chances = (exponent / row_sums).astype(jnp.bfloat16)
        mixture = jnp.einsum(
            "sgqk,ksd->qsgd", chances, value_seq, preferred_element_type=jnp.float32
        )
        log_total = (largest + jnp.log(row_sums))[..., 0]
        return (mixture.reshape(full_len, local_heads, HD).astype(jnp.bfloat16), log_total)

    attn_heads, log_totals = lax.map(attend, (query_heads, key_heads, value_heads, block_ids))
    attended_tokens = lax.all_to_all(attn_heads, "ulysses", split_axis=1, concat_axis=2, tiled=True)
    attended = attended_tokens.reshape(row_total, query_width)
    branch_attn = jnp.dot(attended, out_full, preferred_element_type=jnp.float32)
    middle = inputs_flat + keep_rows * branch_attn
    inv_two = lax.rsqrt(jnp.mean(middle * middle, -1, keepdims=True) + epsilon)
    unit_two = middle * inv_two
    gain_piece = lax.all_gather(mlp_gain, "fsdp", axis=0, tiled=True)
    gate_piece = lax.all_gather(w_gate, "fsdp", axis=0, tiled=True)
    up_piece = lax.all_gather(w_up, "fsdp", axis=0, tiled=True)
    gain_float = gain_piece.astype(jnp.float32)
    normed_piece = (unit_two * gain_float).astype(jnp.bfloat16)
    gate_sum = jnp.dot(normed_piece, gate_piece, preferred_element_type=jnp.float32)
    up_sum = jnp.dot(normed_piece, up_piece, preferred_element_type=jnp.float32)
    sigmoid_gate = jax.nn.sigmoid(gate_sum)
    silu_gate = gate_sum * sigmoid_gate
    hidden = (silu_gate * up_sum).astype(jnp.bfloat16)
    branch_mlp = jnp.dot(
        hidden,
        lax.all_gather(w_down, "fsdp", axis=1, tiled=True),
        preferred_element_type=jnp.float32,
    )
    output = (middle + keep_rows * branch_mlp).astype(jnp.bfloat16).reshape(layer_input.shape)
    grad_out = cotangent.astype(jnp.float32).reshape(row_total, width)
    grad_mlp = (keep_rows * grad_out).astype(jnp.bfloat16)
    grad_hidden = jnp.einsum(
        "rc,fc->rf",
        grad_mlp,
        lax.all_gather(w_down, "fsdp", axis=1, tiled=True),
        preferred_element_type=jnp.float32,
    )
    grad_gate = (
        grad_hidden * up_sum * sigmoid_gate * (1.0 + gate_sum * (1.0 - sigmoid_gate))
    ).astype(jnp.bfloat16)
    grad_up = (grad_hidden * silu_gate).astype(jnp.bfloat16)
    stacked_in = jnp.stack([w_gate, w_up])
    shard_piece = lax.all_gather(stacked_in, "fsdp", axis=1, tiled=True)
    from_gate = jnp.einsum(
        "rf,cf->rc", grad_gate, shard_piece[0], preferred_element_type=jnp.float32
    )
    grad_normed_two = from_gate + jnp.einsum(
        "rf,cf->rc", grad_up, shard_piece[1], preferred_element_type=jnp.float32
    )
    grad_unit_two = grad_normed_two * gain_float
    grad_gain_two = jnp.sum(grad_normed_two * unit_two, 0)
    grad_middle = grad_out + inv_two * (
        grad_unit_two - unit_two * jnp.mean(grad_unit_two * unit_two, -1, keepdims=True)
    )
    grad_branch = (keep_rows * grad_middle).astype(jnp.bfloat16)
    grad_attended = jnp.einsum(
        "rd,cd->rc", grad_branch, out_full, preferred_element_type=jnp.float32
    )
    grad_attended = grad_attended.astype(jnp.bfloat16).reshape(seq_count, local_len, H, HD)
    grad_heads = lax.all_to_all(grad_attended, "ulysses", split_axis=2, concat_axis=1, tiled=True)

    def attend_back(record):
        query_seq, key_seq, value_seq, block_row, log_total, grad_seq = record
        scores = scores_for(query_seq, key_seq, block_row)
        chances = jnp.exp(scores - log_total[..., None])
        grouped = query_seq.reshape(full_len, local_slots, group_size, HD)
        grouped_grad = grad_seq.reshape(full_len, local_slots, group_size, HD)
        grad_chances = jnp.einsum(
            "qsgd,ksd->sgqk", grouped_grad, value_seq, preferred_element_type=jnp.float32
        )
        center = jnp.sum(chances * grad_chances, -1, keepdims=True)
        grad_scores = (chances * (grad_chances - center)).astype(jnp.bfloat16)
        grad_query = (
            jnp.einsum("sgqk,ksd->qsgd", grad_scores, key_seq, preferred_element_type=jnp.float32)
            * head_scale
        )
        grad_key = (
            jnp.einsum("sgqk,qsgd->ksd", grad_scores, grouped, preferred_element_type=jnp.float32)
            * head_scale
        )
        grad_value = jnp.einsum(
            "sgqk,qsgd->ksd",
            chances.astype(jnp.bfloat16),
            grouped_grad,
            preferred_element_type=jnp.float32,
        )
        return (
            grad_query.reshape(full_len, local_heads, HD).astype(jnp.bfloat16),
            grad_key.astype(jnp.bfloat16),
            grad_value.astype(jnp.bfloat16),
        )

    grad_query_heads, grad_key_heads, grad_value_heads = lax.map(
        attend_back, (query_heads, key_heads, value_heads, block_ids, log_totals, grad_heads)
    )
    grad_query_tok, grad_key_tok, grad_value_tok = (
        lax.all_to_all(grad_query_heads, "ulysses", split_axis=1, concat_axis=2, tiled=True),
        lax.all_to_all(grad_key_heads, "ulysses", split_axis=1, concat_axis=2, tiled=True),
        lax.all_to_all(grad_value_heads, "ulysses", split_axis=1, concat_axis=2, tiled=True),
    )
    grad_key_sum = (
        grad_key_tok.astype(jnp.float32).reshape(seq_count, local_len, KVH, repeat_count, HD).sum(3)
    )
    grad_value_sum = (
        grad_value_tok.astype(jnp.float32)
        .reshape(seq_count, local_len, KVH, repeat_count, HD)
        .sum(3)
    )
    grad_query_pre = (
        unrotate(grad_query_tok.astype(jnp.float32), cosine, sine_table)
        .astype(jnp.bfloat16)
        .reshape(row_total, query_width)
    )
    grad_key_pre = (
        unrotate(grad_key_sum, cosine, sine_table)
        .astype(jnp.bfloat16)
        .reshape(row_total, pair_width)
    )
    grad_value_pre = grad_value_sum.astype(jnp.bfloat16).reshape(row_total, pair_width)
    grad_normed_one = jnp.einsum(
        "rc,dc->rd", grad_query_pre, query_full, preferred_element_type=jnp.float32
    )
    grad_normed_one = grad_normed_one + jnp.einsum(
        "rc,dc->rd", grad_key_pre, key_full, preferred_element_type=jnp.float32
    )
    grad_normed_one = grad_normed_one + jnp.einsum(
        "rc,dc->rd", grad_value_pre, value_full, preferred_element_type=jnp.float32
    )
    grad_unit_one = grad_normed_one * gain_one.astype(jnp.float32)
    grad_gain_one = jnp.sum(grad_normed_one * unit_one, 0)
    grad_input = grad_middle + inv_one * (
        grad_unit_one - unit_one * jnp.mean(grad_unit_one * unit_one, -1, keepdims=True)
    )
    grad_input = grad_input.astype(jnp.bfloat16).reshape(layer_input.shape)
    gain_totals = lax.psum(jnp.stack([grad_gain_one, grad_gain_two]), ("fsdp", "ulysses"))
    owner_rows = width // fsdp_size
    gain_shard = lax.dynamic_slice_in_dim(
        gain_totals, lax.axis_index("fsdp") * owner_rows, owner_rows, 1
    )
    grad_attn_mid = jnp.concatenate([grad_query_pre, grad_key_pre, grad_value_pre], 1)
    grad_mlp_mid = jnp.concatenate([grad_gate, grad_up], 1)
    owner_sums = lax.psum_scatter(
        jnp.concatenate(
            [
                jnp.einsum(
                    "rc,re->ce", normed_one, grad_attn_mid, preferred_element_type=jnp.float32
                ),
                jnp.einsum("rc,re->ce", attended, grad_branch, preferred_element_type=jnp.float32),
                jnp.einsum(
                    "rc,re->ce", normed_piece, grad_mlp_mid, preferred_element_type=jnp.float32
                ),
                jnp.einsum("rc,re->ce", grad_mlp, hidden, preferred_element_type=jnp.float32),
            ],
            1,
        ).astype(jnp.bfloat16),
        "fsdp",
        scatter_dimension=0,
        tiled=True,
    ).astype(jnp.float32)
    owner_sums = lax.psum(owner_sums.astype(jnp.bfloat16), "ulysses").astype(jnp.float32)
    first_value = query_width + pair_width
    first_out = first_value + pair_width
    first_gate = first_out + width
    first_up = first_gate + hidden_width
    first_down = first_up + hidden_width
    return (
        output,
        grad_input,
        gain_shard[0],
        owner_sums[:, :query_width],
        owner_sums[:, query_width:first_value],
        owner_sums[:, first_value:first_out],
        owner_sums[:, first_out:first_gate],
        gain_shard[1],
        owner_sums[:, first_gate:first_up],
        owner_sums[:, first_up:first_down],
        owner_sums[:, first_down : first_down + hidden_width].T,
    )


def solution(mesh):
    return jax.shard_map(
        on_device,
        mesh=mesh,
        in_specs=(
            P("fsdp", "ulysses", None),
            P("fsdp", "ulysses", None),
            P("fsdp", "ulysses"),
            P("fsdp", None),
            P("fsdp"),
            P("fsdp"),
            P("fsdp", None),
            P("fsdp", None),
            P("fsdp", None),
            P("fsdp", None),
            P("fsdp"),
            P("fsdp", None),
            P("fsdp", None),
            P(None, "fsdp"),
        ),
        out_specs=(
            P("fsdp", "ulysses", None),
            P("fsdp", "ulysses", None),
            P("fsdp"),
            P("fsdp", None),
            P("fsdp", None),
            P("fsdp", None),
            P("fsdp", None),
            P("fsdp"),
            P("fsdp", None),
            P("fsdp", None),
            P(None, "fsdp"),
        ),
        check_vma=False,
    )
```

profile of v0, /device:TPU:0, one launch (start us, length us, event | category | flops | bytes accessed | tf_op | source)
XLA Modules:
  0.0 2315.7 jit_solution(7480973175895499666)
XLA Ops:
  55.5 14.9 all-gather.13.cloned.1.call-done
  79.3 47.4 %all-gather.15.cloned.1.call-done = bf16[2048,2048]{1,0:T(8,128)(2,1)} async-done(((bf16[256,2048]{1,0:T(8,128)(2,1)}), bf16[2048,2048]{1,0:T(8,128)(2,1)}) %all-gather.15.cloned.1.call-update) | async-done | bytes 8388624 | tf_op jit(solution)/shard_map/all_gather | solution.py:64
  126.7 12.4 copy.162
  172.7 66.7 %all-to-all-done.2 = bf16[3,256,16,128]{1,3,0,2:T(8,128)(2,1)} async-done(((bf16[3,256,16,128]{1,3,0,2:T(8,128)(2,1)}), bf16[3,256,16,128]{1,3,0,2:T(8,128)(2,1)}, u32[]{:S(2)}, u32[]{:S(2)}) %all-to-all-start.2) | async-done | bytes 3145760 | tf_op jit(solution)/shard_map/all_to_all | solution.py:90
  246.5 55.1 %while.26 = (s32[]{:T(128)}, bf16[3,1024,4,128]{3,2,0,1:T(4,128)(2,1)}, f32[3,1,4,1024]{3,2,1,0:T(4,128)}, bf16[3,1024,1,128]{3,1,0,2:T(8,128)(2,1)}, s32[3,1024...) while((s32[]{:T(128)}, ...), condition=%wide.region_4.5_spmd, body=%wide.region_1.4_spmd.sunk | while | flops 2199384064 | bytes 61486188 | solution.py:121
  319.6 57.0 %all-to-all-done.3 = bf16[3,1024,4,128]{3,2,0,1:T(4,128)(2,1)} async-done(((bf16[3,1024,4,128]{3,2,0,1:T(4,128)(2,1)}), bf16[3,1024,4,128]{3,2,0,1:T(4,128)(2,1)}, u32[]{:S(2)}, u32[]{:S(2)}) %all-to-all-start.3) | async-done | bytes 3145760 | tf_op jit(solution)/shard_map/all_to_all | solution.py:122
  387.7 10.5 multiply_reduce_fusion.2
  401.5 26.0 %fusion.115 = f32[768,5632]{1,0:T(8,128)} fusion(bf16[768,2048]{1,0:T(8,128)(2,1)S(1)} %multiply_convert_fusion.5, bf16[2048,5632]{1,0:T(8,128)(2,1)} %all-gather.21.cloned.1.call-done), kind=kOutput, calls=%fused_computation.174 | convolution fusion | flops 17716740096 | bytes 43515904 | tf_op jit(solution)/shard_map/dot_general | solution.py:134
  427.6 25.9 %fusion.116 = f32[768,5632]{1,0:T(8,128)} fusion(bf16[768,2048]{1,0:T(8,128)(2,1)} %fusion.73, bf16[5632,2048]{1,0:T(8,128)(2,1)} %all-gather.23.cloned.1.call-done), kind=kOutput, calls=%fused_computation.175 | convolution fusion | flops 17716740096 | bytes 43515904 | tf_op jit(solution)/shard_map/rc,fc->rf/dot_general | solution.py:146
  453.5 88.7 %all-gather.19.cloned.1.call-done = bf16[2048,5632]{1,0:T(8,128)(2,1)} async-done(((bf16[256,5632]{1,0:T(8,128)(2,1)}), bf16[2048,5632]{1,0:T(8,128)(2,1)}) %all-gather.19.cloned.1.call-update) | async-done | bytes 23068688 | tf_op jit(solution)/shard_map/all_gather | solution.py:129
  542.2 40.9 %multiply_convert_fusion.2 = (bf16[768,5632]{1,0:T(8,128)(2,1)}, bf16[768,5632]{1,0:T(8,128)(2,1)}, bf16[768,5632]{1,0:T(8,128)(2,1)}) fusion(f32[768,5632]{1,0:T(8,128)} %fusion.116, f32[768,5632]{1,0:T(8,128)} %fusion.115, bf16[768,2048]{1,0:T(8,128)(2,1)S(1)} %multiply_convert_fusion.5, bf16[2048,5632]{1,0:T(8,128)(2,1)} %all-gather.19.cloned.1.call-done), kind=kOutput, calls=%fused_computation.82 | convolution fusion | flops 17781620736 | bytes 86769664 | tf_op jit(solution)/shard_map/dot_general | solution.py:133
  583.1 175.8 %all-gather.25.cloned.1.call-done = bf16[2,2048,5632]{2,1,0:T(8,128)(2,1)} async-done(((bf16[2,256,5632]{2,1,0:T(8,128)(2,1)}), bf16[2,2048,5632]{2,1,0:T(8,128)(2,1)}) %all-gather.25.cloned.1.call-update) | async-done | bytes 46137360 | tf_op jit(solution)/shard_map/all_gather | solution.py:157
  758.8 25.1 %fusion.67 = f32[768,2048]{1,0:T(8,128)} fusion(bf16[768,5632]{1,0:T(8,128)(2,1)} %get-tuple-element.291, bf16[2,2048,5632]{2,1,0:T(8,128)(2,1)} %all-gather.25.cloned.1.call-done), kind=kOutput, calls=%fused_computation.74 | convolution fusion | flops 17716740096 | bytes 38010880 | tf_op jit(solution)/shard_map/rf,cf->rc/dot_general | solution.py:161
  784.0 27.1 %multiply_reduce_fusion = (f32[2048]{0:T(1024)}, f32[768]{0:T(1024)S(1)}, f32[768,2048]{1,0:T(8,128)}) fusion(f32[768,2048]{1,0:T(8,128)S(1)} %copy-done.8, f32[768]{0:T(1024)S(1)} %copy-done.31, f32[2048]{0:T(1024)S(1)} %bitcast.438, f32[768,2048]{1,0:T(8,128)} %fusion.67, bf16[768,5632]{1,0:T(8,128)(2,1)} %get-tuple-element.290, ...), kind=kOutput, calls=%fused_computation.117 | convolution fusion | flops 17727748096 | bytes 50616320 | tf_op jit(solution)/shard_map/rf,cf->rc/dot_general | solution.py:158
  815.7 11.4 fusion.98
  835.2 71.1 %all-to-all-done.4 = bf16[3,256,16,128]{3,1,0,2:T(8,128)(2,1)S(1)} async-done(((bf16[3,256,16,128]{3,1,0,2:T(8,128)(2,1)}), bf16[3,256,16,128]{3,1,0,2:T(8,128)(2,1)S(1)}, u32[]{:S(2)}, u32[]{:S(2)}) %all-to-all-start.4) | async-done | bytes 3145760 | tf_op jit(solution)/shard_map/all_to_all | solution.py:174
  912.5 179.5 %while.27 = (s32[]{:T(128)}, bf16[3,1024,4,128]{3,2,0,1:T(4,128)(2,1)}, bf16[3,1024,1,128]{1,3,2,0:T(8,128)(2,1)}, bf16[3,1024,1,128]{1,3,2,0:T(8,128)(2,1)}, bf...) while((s32[]{:T(128)}, ...), condition=%wide.region_9.10_spmd, body=%wide.region_7.9_spmd.sunk | while | flops 5408944128 | bytes 264601872 | solution.py:207
  934.3 13.6 fusion.185
  994.0 13.6 fusion.185
  1053.7 13.6 fusion.185
  1102.7 20.5 all-to-all-done.7
  1126.7 44.9 %convolution_convert_fusion = bf16[2048,11264]{1,0:T(8,128)(2,1)} fusion(bf16[768,2048]{1,0:T(8,128)(2,1)} %copy-done.22, bf16[768,5632]{1,0:T(8,128)(2,1)} %get-tuple-element.291, bf16[768,5632]{1,0:T(8,128)(2,1)} %get-tuple-element.290), kind=kOutput, calls=%fused_computation.72 | convolution fusion | flops 35491151872 | bytes 66584576 | tf_op jit(solution)/shard_map/rc,re->ce/dot_general | solution.py:263
  1177.6 26.4 %convolution_convert_fusion.1 = bf16[2048,5632]{1,0:T(8,128)(2,1)} fusion(bf16[768,2048]{1,0:T(8,128)(2,1)} %fusion.73, bf16[768,5632]{1,0:T(8,128)(2,1)} %get-tuple-element.292), kind=kOutput, calls=%fused_computation.77 | convolution fusion | flops 17728274432 | bytes 34865152 | tf_op jit(solution)/shard_map/rc,re->ce/dot_general | solution.py:266
  1204.0 12.2 convolution_convert_fusion.3
  1216.2 12.3 copy.187
  1305.7 10.9 fusion.117
  1327.1 13.4 convolution_convert_fusion.2
  1340.5 59.2 %pad_maximum_fusion = bf16[2048,22016]{1,0:T(8,128)(2,1)} fusion(bf16[2048,5632]{1,0:T(8,128)(2,1)} %convolution_convert_fusion.1, bf16[2048,11264]{1,0:T(8,128)(2,1)} %convolution_convert_fusion, bf16[2048,2048]{1,0:T(8,128)(2,1)} %copy.187, bf16[2048,3072]{1,0:T(8,128)(2,1)} %convolution_convert_fusion.2), kind=kLoop, calls=%fused_computation.71 | loop fusion | flops 360710144 | bytes 180355072 | tf_op jit(solution)/shard_map/concatenate | solution.py:257
  1399.8 490.7 %reduce-scatter.4.cloned.1.call-done = bf16[256,22016]{1,0:T(8,128)(2,1)} async-done(((bf16[2048,22016]{1,0:T(8,128)(2,1)}), bf16[256,22016]{1,0:T(8,128)(2,1)}) %reduce-scatter.4.cloned.1.call-update) | async-done | bytes 11272208
  1890.6 25.1 %add_convert_fusion = bf16[768,2048]{1,0:T(8,128)(2,1)} fusion(f32[768,2048]{1,0:T(8,128)} %copy-done.7, bf16[768,5632]{1,0:T(8,128)(2,1)} %get-tuple-element.292, bf16[5632,2048]{1,0:T(8,128)(2,1)} %all-gather.23.cloned.1.call-done, f32[768]{0:T(1024)S(1)} %copy-done.38), kind=kOutput, calls=%fused_computation.121 | convolution fusion | flops 17721458688 | bytes 41159680 | tf_op jit(solution)/shard_map/dot_general | solution.py:138
  1915.7 44.5 %psum.14 = f32[2,2048]{1,0:T(2,128)S(1)} all-reduce(f32[2,2048]{1,0:T(2,128)S(1)} %pad_maximum_fusion.6), channel_id=1, replica_groups=mesh['fsdp'=8,'ulysses'=4] {'fsdp','ulysses'}, use_global_device_ids=true, to_apply=%region_13.14 | all-reduce | flops 4096 | bytes 32768 | tf_op jit(solution)/shard_map/psum | solution.py:249
  1960.9 316.9 %all-reduce.3.cloned.1.call-done = bf16[256,22016]{1,0:T(8,128)(2,1)} async-done(((bf16[256,22016]{1,0:T(8,128)(2,1)}), bf16[256,22016]{1,0:T(8,128)(2,1)}) %all-reduce.3.cloned.1.call-update) | async-done | bytes 11272208 | tf_op jit(solution)/shard_map/psum | solution.py:274
  (283 shorter events, 481.2 us)
Async XLA Ops:
  7.2 33.4 %all-gather.11.cloned.1.call-start = ((), (), s32[]{:S(2)}) async-start(), calls=%async_computation.9 | async-start | bytes 2359296 | tf_op jit(solution)/shard_map/all_gather | solution.py:66
  7.9 62.5 %all-gather.13.cloned.1.call-start = ((), (), s32[]{:S(2)}) async-start(), calls=%async_computation.10 | async-start | bytes 2359296 | tf_op jit(solution)/shard_map/all_gather | solution.py:65
  8.7 118.0 %all-gather.15.cloned.1.call-start = ((), (), s32[]{:S(2)}) async-start(), calls=%async_computation.11 | async-start | bytes 9437184 | tf_op jit(solution)/shard_map/all_gather | solution.py:64
  9.4 378.3 %all-gather.17.cloned.1.call-start = ((), (), s32[]{:S(2)}) async-start(), calls=%async_computation.12 | async-start | bytes 9437184 | tf_op jit(solution)/shard_map/all_gather | solution.py:67
  10.0 391.6 %all-gather.21.cloned.1.call-start = ((), (), s32[]{:S(2)}) async-start(), calls=%async_computation.14 | async-start | bytes 25952256 | tf_op jit(solution)/shard_map/all_gather | solution.py:130
  10.6 417.0 %all-gather.23.cloned.1.call-start = ((), (), s32[]{:S(2)}) async-start(), calls=%async_computation.15 | async-start | bytes 25952256 | tf_op jit(solution)/shard_map/all_gather | solution.py:140
  11.1 531.1 %all-gather.19.cloned.1.call-start = ((), (), s32[]{:S(2)}) async-start(), calls=%async_computation.13 | async-start | bytes 25952256 | tf_op jit(solution)/shard_map/all_gather | solution.py:129
  11.9 746.9 %all-gather.25.cloned.1.call-start = ((), (), s32[]{:S(2)}) async-start(), calls=%async_computation.16 | async-start | bytes 51904512 | tf_op jit(solution)/shard_map/all_gather | solution.py:157
  28.3 115.3 %copy-start.26 = (f32[8,1,256]{2,1,0:T(1,128)}, f32[8,1,256]{2,1,0:T(1,128)S(1)}, u32[]{:S(2)}) copy-start(f32[8,1,256]{2,1,0:T(1,128)S(1)} %convert_element_type.245) | copy-start | bytes 24580
  29.0 114.6 %copy-start.33 = (f32[3,256]{1,0:T(4,128)}, f32[3,256]{1,0:T(4,128)S(1)}, u32[]{:S(2)}) copy-start(f32[3,256]{1,0:T(4,128)S(1)} %add_rsqrt_fusion.1) | copy-start | bytes 9220
  48.8 90.2 %all-to-all-start = ((bf16[3,256,4,128]{3,1,0,2:T(8,128)(2,1)}), bf16[3,256,4,128]{3,1,0,2:T(8,128)(2,1)}, u32[]{:S(2)}, u32[]{:S(2)}) async-start(bf16[3,256,4,128]{3,1,0,2:T(8,128)(2,1)} %copy.157), calls=%async_computation | async-start | bytes 1572864 | tf_op jit(solution)/shard_map/all_to_all | solution.py:92
  55.5 98.4 %copy-start.12 = (f32[3,256,128]{1,2,0:T(8,128)}, f32[3,256,128]{1,2,0:T(8,128)S(1)}, u32[]{:S(2)}) copy-start(f32[3,256,128]{1,2,0:T(8,128)S(1)} %get-tuple-element.318) | copy-start | bytes 1179652
  139.1 25.2 %all-to-all-start.1 = ((bf16[3,256,4,128]{1,3,0,2:T(8,128)(2,1)}), bf16[3,256,4,128]{1,3,0,2:T(8,128)(2,1)}, u32[]{:S(2)}, u32[]{:S(2)}) async-start(bf16[3,256,4,128]{1,3,0,2:T(8,128)(2,1)} %copy.160), calls=%async_computation.1 | async-start | bytes 1572864 | tf_op jit(solution)/shard_map/all_to_all | solution.py:91
  164.3 75.1 %all-to-all-start.2 = ((bf16[3,256,16,128]{1,3,0,2:T(8,128)(2,1)}), bf16[3,256,16,128]{1,3,0,2:T(8,128)(2,1)}, u32[]{:S(2)}, u32[]{:S(2)}) async-start(bf16[3,256,16,128]{1,3,0,2:T(8,128)(2,1)} %copy.163), calls=%async_computation.2 | async-start | bytes 6291456 | tf_op jit(solution)/shard_map/all_to_all | solution.py:90
  301.6 75.0 %all-to-all-start.3 = ((bf16[3,1024,4,128]{3,2,0,1:T(4,128)(2,1)}), bf16[3,1024,4,128]{3,2,0,1:T(4,128)(2,1)}, u32[]{:S(2)}, u32[]{:S(2)}) async-start(bf16[3,1024,4,128]{3,2,0,1:T(4,128)(2,1)} %get-tuple-element.103), calls=%async_computation.3 | async-start | bytes 6291456 | tf_op jit(solution)/shard_map/all_to_all | solution.py:122
  306.5 81.2 %copy-start.35 = (f32[768]{0:T(1024)}, f32[768]{0:T(1024)S(1)}, u32[]{:S(2)}) copy-start(f32[768]{0:T(1024)S(1)} %mul.276) | copy-start | bytes 9220
  315.4 82.9 %copy-start.28 = (f32[8,1,256]{2,1,0:T(1,128)}, f32[8,1,256]{2,1,0:T(1,128)S(1)}, u32[]{:S(2)}) copy-start(f32[8,1,256]{2,1,0:T(1,128)S(1)} %convert_element_type.246) | copy-start | bytes 24580
  401.5 140.7 %copy-start.22 = (bf16[768,2048]{1,0:T(8,128)(2,1)}, bf16[768,2048]{1,0:T(8,128)(2,1)S(1)}, u32[]{:S(2)}) copy-start(bf16[768,2048]{1,0:T(8,128)(2,1)S(1)} %multiply_convert_fusion.5) | copy-start | bytes 9437188
  758.8 25.2 %copy-start.8 = (f32[768,2048]{1,0:T(8,128)S(1)}, f32[768,2048]{1,0:T(8,128)}, u32[]{:S(2)}) copy-start(f32[768,2048]{1,0:T(8,128)} %copy-done.7) | copy-start | bytes 18874372
  758.8 25.2 %copy-start.29 = (f32[8,1,256]{2,1,0:T(1,128)S(1)}, f32[8,1,256]{2,1,0:T(1,128)}, u32[]{:S(2)}) copy-start(f32[8,1,256]{2,1,0:T(1,128)} %copy-done.28) | copy-start | bytes 24580
  758.8 25.2 %copy-start.31 = (f32[768]{0:T(1024)S(1)}, f32[768]{0:T(1024)}, u32[]{:S(2)}) copy-start(f32[768]{0:T(1024)} %copy-done.30) | copy-start | bytes 9220
  830.6 75.7 %all-to-all-start.4 = ((bf16[3,256,16,128]{3,1,0,2:T(8,128)(2,1)}), bf16[3,256,16,128]{3,1,0,2:T(8,128)(2,1)S(1)}, u32[]{:S(2)}, u32[]{:S(2)}) async-start(bf16[3,256,16,128]{3,1,0,2:T(8,128)(2,1)} %copy.169), calls=%async_computation.4 | async-start | bytes 6291456 | tf_op jit(solution)/shard_map/all_to_all | solution.py:174
  912.5 185.3 %copy-start.34 = (f32[3,256]{1,0:T(4,128)S(1)}, f32[3,256]{1,0:T(4,128)}, u32[]{:S(2)}) copy-start(f32[3,256]{1,0:T(4,128)} %copy-done.33) | copy-start | bytes 9220
  1094.4 28.8 %all-to-all-start.7 = ((bf16[3,1024,1,128]{3,0,2,1:T(4,128)(2,1)}), bf16[3,1024,1,128]{3,0,2,1:T(4,128)(2,1)S(1)}, u32[]{:S(2)}, u32[]{:S(2)}) async-start(bf16[3,1024,1,128]{3,0,2,1:T(4,128)(2,1)} %copy.184), calls=%async_computation.7 | async-start | bytes 2097152 | tf_op jit(solution)/shard_map/all_to_all | solution.py:213
  1123.2 48.5 %copy-start.19 = (bf16[3,1024,1,128]{3,0,2,1:T(4,128)(2,1)}, bf16[3,1024,1,128]{3,0,2,1:T(4,128)(2,1)S(1)}, u32[]{:S(2)}) copy-start(bf16[3,1024,1,128]{3,0,2,1:T(4,128)(2,1)S(1)} %all-to-all-done.7) | copy-start | bytes 2359300
  1123.2 48.5 %all-to-all-start.6 = ((bf16[3,1024,1,128]{3,0,2,1:T(4,128)(2,1)}), bf16[3,1024,1,128]{3,0,2,1:T(4,128)(2,1)S(1)}, u32[]{:S(2)}, u32[]{:S(2)}) async-start(bf16[3,1024,1,128]{3,0,2,1:T(4,128)(2,1)} %copy.178), calls=%async_computation.6 | async-start | bytes 2097152 | tf_op jit(solution)/shard_map/all_to_all | solution.py:212
  1172.6 82.8 %all-to-all-start.5 = ((bf16[3,1024,4,128]{3,2,0,1:T(4,128)(2,1)}), bf16[3,1024,4,128]{3,2,0,1:T(4,128)(2,1)S(1)}, u32[]{:S(2)}, u32[]{:S(2)}) async-start(bf16[3,1024,4,128]{3,2,0,1:T(4,128)(2,1)} %get-tuple-element.105), calls=%async_computation.5 | async-start | bytes 6291456 | tf_op jit(solution)/shard_map/all_to_all | solution.py:211
  1177.6 712.9 %reduce-scatter.4.cloned.1.call-start = ((), (), s32[]{:S(2)}) async-start(), calls=%async_computation.18 | async-start | bytes 101449728
  1177.6 26.4 %copy-start.37 = (f32[768]{0:T(1024)S(1)}, f32[768]{0:T(1024)}, u32[]{:S(2)}) copy-start(f32[768]{0:T(1024)} %copy-done.35) | copy-start | bytes 9220
  1399.8 490.8 %copy-start.38 = (f32[768]{0:T(1024)S(1)}, f32[768]{0:T(1024)}, u32[]{:S(2)}) copy-start(f32[768]{0:T(1024)} %copy-done.35) | copy-start | bytes 9220
  1399.8 878.0 %all-reduce.3.cloned.1.call-start = ((), (), s32[]{:S(2)}) async-start(), calls=%async_computation.17 | async-start | bytes 22544384 | tf_op jit(solution)/shard_map/psum | solution.py:274
  1890.6 25.1 %copy-start.39 = (f32[2048]{0:T(1024)S(1)}, f32[2048]{0:T(1024)}, u32[]{:S(2)}) copy-start(f32[2048]{0:T(1024)} %get-tuple-element.248) | copy-start | bytes 24580
  (40 other events, 328.3 us)
Sparse Core Ops, SparseCore 0:
  9.9 30.6 all-gather.10
  42.4 27.8 all-gather.12
  72.3 54.3 all-gather.14
  128.4 54.3 all-gather.16
  184.6 116.4 all-gather.20
  302.8 120.9 all-gather.22
  425.7 116.4 all-gather.18
  544.7 214.1 all-gather.24
  1399.9 490.6 reduce-scatter.3
  1892.9 384.8 all-reduce.2
where the time goes:
time: 2330 us; the launch traced here: 2320 us
  waiting for transfers between devices  1370 us (59%)
  matrix products  471 us (20%)
  other arithmetic  181 us (8%)
  local copies, waits for them, and re-layouts  178 us (8%)
  blocking collectives  63.7 us (3%)
  starting transfers between devices  35.7 us (2%)
    unnamed x11, waiting for transfers between devices  495 us
    psum x1, waiting for transfers between devices, on_device(): lax.psum(owner_sums.astype(jnp.bfloat16), 'ulysses').astype(jnp.float32)  317 us
    all_gather x1, waiting for transfers between devices, on_device(): shard_piece = lax.all_gather(stacked_in, 'fsdp', axis=1, tiled=True)  176 us
    all_gather x1, waiting for transfers between devices, on_device(): gate_piece = lax.all_gather(w_gate, 'fsdp', axis=0, tiled=True)  88.7 us
    all_to_all x1, waiting for transfers between devices, on_device(): lax.all_to_all(grad_attended, 'ulysses', split_axis=2, concat_axis=1, til...  71.1 us
    all_to_all x1, waiting for transfers between devices, on_device(): lax.all_to_all(query_sent, 'ulysses', split_axis=2, concat_axis=1, tiled=...  66.7 us
    concatenate x1, other arithmetic, on_device(): jnp.concatenate([jnp.einsum('rc,re->ce', normed_one, grad_attn_mid, prefe...  59.2 us
    all_to_all x1, waiting for transfers between devices, on_device(): lax.all_to_all(attn_heads, 'ulysses', split_axis=1, concat_axis=2, tiled=...  57 us
  transfers between devices with their start and end apart: 18, of which 12 were waited for; matrix products, arithmetic and copies ran while one was open for 17% of the time, Pallas kernels for 0%

commit v1 on v0

--- a/solution.py
+++ b/solution.py
@@ -271,7 +271,9 @@
         scatter_dimension=0,
         tiled=True,
     ).astype(jnp.float32)
-    owner_sums = lax.psum(owner_sums.astype(jnp.bfloat16), "ulysses").astype(jnp.float32)
+    owner_sums = jnp.sum(lax.all_gather(owner_sums.astype(jnp.bfloat16), "ulysses"), axis=0).astype(
+        jnp.float32
+    )
     first_value = query_width + pair_width
     first_out = first_value + pair_width
     first_gate = first_out + width

time: 2330 us -> 2730 us (1.17)
  waiting for transfers between devices: 1370 us -> 1710 us
  other arithmetic: 181 us -> 213 us
  blocking collectives: 63.7 us -> 91.9 us
    all_gather x0 -> x1, waiting for transfers between devices: none -> 653 us  [on_device(): lax.all_gather(owner_sums.astype(jnp.bfloat16), 'ulysses')]
    psum x1 -> x0, waiting for transfers between devices: 317 us -> none  [on_device(): lax.psum(owner_sums.astype(jnp.bfloat16), 'ulysses').astype(jnp.float32)]
    reduce_sum x0 -> x1, other arithmetic: none -> 30.4 us  [on_device(): jnp.sum(lax.all_gather(owner_sums.astype(jnp.bfloat16), 'ulysses'), axis=0)]
    psum x1, blocking collectives: 44.5 us -> 72.8 us  [on_device(): lax.psum(jnp.stack([grad_gain_one, grad_gain_two]), ('fsdp', 'ulysses'))]
  transfers between devices with their start and end apart: 18 -> 18, of which waited for: 12 -> 12; matrix products, arithmetic and copies ran while one was open for 17% -> 14% of each run, Pallas kernels for 0% -> 0%
where the time goes in v1:
time: 2730 us; the launch traced here: 2720 us
  waiting for transfers between devices  1710 us (63%)
  matrix products  473 us (17%)
  other arithmetic  213 us (8%)
  local copies, waits for them, and re-layouts  180 us (7%)
  blocking collectives  91.9 us (3%)
  starting transfers between devices  35.7 us (1%)
    all_gather x1, waiting for transfers between devices, on_device(): lax.all_gather(owner_sums.astype(jnp.bfloat16), 'ulysses')  653 us
    unnamed x11, waiting for transfers between devices  495 us
    all_gather x1, waiting for transfers between devices, on_device(): shard_piece = lax.all_gather(stacked_in, 'fsdp', axis=1, tiled=True)  176 us
    all_gather x1, waiting for transfers between devices, on_device(): gate_piece = lax.all_gather(w_gate, 'fsdp', axis=0, tiled=True)  88.6 us
    psum x1, blocking collectives, on_device(): lax.psum(jnp.stack([grad_gain_one, grad_gain_two]), ('fsdp', 'ulysses'))  72.8 us
    all_to_all x1, waiting for transfers between devices, on_device(): lax.all_to_all(grad_attended, 'ulysses', split_axis=2, concat_axis=1, til...  71.1 us
    all_to_all x1, waiting for transfers between devices, on_device(): lax.all_to_all(query_sent, 'ulysses', split_axis=2, concat_axis=1, tiled=...  66.7 us
    concatenate x1, other arithmetic, on_device(): jnp.concatenate([jnp.einsum('rc,re->ce', normed_one, grad_attn_mid, prefe...  59.3 us
  transfers between devices with their start and end apart: 18, of which 12 were waited for; matrix products, arithmetic and copies ran while one was open for 14% of the time, Pallas kernels for 0%

profile of v1, /device:TPU:0, one launch (start us, length us, event | category | flops | bytes accessed | tf_op | source)
XLA Modules:
  0.0 2716.4 jit_solution(1754007842304552236)
XLA Ops:
  55.5 14.9 all-gather.15.cloned.1.call-done
  79.3 47.4 %all-gather.17.cloned.1.call-done = bf16[2048,2048]{1,0:T(8,128)(2,1)} async-done(((bf16[256,2048]{1,0:T(8,128)(2,1)}), bf16[2048,2048]{1,0:T(8,128)(2,1)}) %all-gather.17.cloned.1.call-update) | async-done | bytes 8388624 | tf_op jit(solution)/shard_map/all_gather | solution.py:64
  126.7 12.4 copy.172
  172.7 66.7 %all-to-all-done.2 = bf16[3,256,16,128]{1,3,0,2:T(8,128)(2,1)} async-done(((bf16[3,256,16,128]{1,3,0,2:T(8,128)(2,1)}), bf16[3,256,16,128]{1,3,0,2:T(8,128)(2,1)}, u32[]{:S(2)}, u32[]{:S(2)}) %all-to-all-start.2) | async-done | bytes 3145760 | tf_op jit(solution)/shard_map/all_to_all | solution.py:90
  246.5 55.1 %while.26 = (s32[]{:T(128)}, bf16[3,1024,4,128]{3,2,0,1:T(4,128)(2,1)}, f32[3,1,4,1024]{3,2,1,0:T(4,128)}, bf16[3,1024,1,128]{3,1,0,2:T(8,128)(2,1)}, s32[3,1024...) while((s32[]{:T(128)}, ...), condition=%wide.region_4.5_spmd, body=%wide.region_1.4_spmd.sunk | while | flops 2199384064 | bytes 61486188 | solution.py:121
  319.6 57.0 %all-to-all-done.3 = bf16[3,1024,4,128]{3,2,0,1:T(4,128)(2,1)} async-done(((bf16[3,1024,4,128]{3,2,0,1:T(4,128)(2,1)}), bf16[3,1024,4,128]{3,2,0,1:T(4,128)(2,1)}, u32[]{:S(2)}, u32[]{:S(2)}) %all-to-all-start.3) | async-done | bytes 3145760 | tf_op jit(solution)/shard_map/all_to_all | solution.py:122
  401.5 26.1 fusion.115
  427.6 26.0 fusion.116
  453.6 88.6 %all-gather.21.cloned.1.call-done = bf16[2048,5632]{1,0:T(8,128)(2,1)} async-done(((bf16[256,5632]{1,0:T(8,128)(2,1)}), bf16[2048,5632]{1,0:T(8,128)(2,1)}) %all-gather.21.cloned.1.call-update) | async-done | bytes 23068688 | tf_op jit(solution)/shard_map/all_gather | solution.py:129
  542.2 40.7 %multiply_convert_fusion.2 = (bf16[768,5632]{1,0:T(8,128)(2,1)}, bf16[768,5632]{1,0:T(8,128)(2,1)}, bf16[768,5632]{1,0:T(8,128)(2,1)}) fusion(f32[768,5632]{1,0:T(8,128)} %fusion.116, f32[768,5632]{1,0:T(8,128)} %fusion.115, bf16[768,2048]{1,0:T(8,128)(2,1)S(1)} %multiply_convert_fusion.5, bf16[2048,5632]{1,0:T(8,128)(2,1)} %all-gather.21.cloned.1.call-done), kind=kOutput, calls=%fused_computation.82 | convolution fusion | flops 17781620736 | bytes 86769664 | tf_op jit(solution)/shard_map/dot_general | solution.py:133
  582.9 175.9 %all-gather.27.cloned.1.call-done = bf16[2,2048,5632]{2,1,0:T(8,128)(2,1)} async-done(((bf16[2,256,5632]{2,1,0:T(8,128)(2,1)}), bf16[2,2048,5632]{2,1,0:T(8,128)(2,1)}) %all-gather.27.cloned.1.call-update) | async-done | bytes 46137360 | tf_op jit(solution)/shard_map/all_gather | solution.py:157
  758.8 25.2 fusion.67
  784.0 27.1 multiply_reduce_fusion
  815.8 11.4 fusion.98
  835.3 71.1 %all-to-all-done.4 = bf16[3,256,16,128]{3,1,0,2:T(8,128)(2,1)S(1)} async-done(((bf16[3,256,16,128]{3,1,0,2:T(8,128)(2,1)}), bf16[3,256,16,128]{3,1,0,2:T(8,128)(2,1)S(1)}, u32[]{:S(2)}, u32[]{:S(2)}) %all-to-all-start.4) | async-done | bytes 3145760 | tf_op jit(solution)/shard_map/all_to_all | solution.py:174
  912.6 179.6 %while.27 = (s32[]{:T(128)}, bf16[3,1024,4,128]{3,2,0,1:T(4,128)(2,1)}, bf16[3,1024,1,128]{1,3,2,0:T(8,128)(2,1)}, bf16[3,1024,1,128]{1,3,2,0:T(8,128)(2,1)}, bf...) while((s32[]{:T(128)}, ...), condition=%wide.region_9.10_spmd, body=%wide.region_7.9_spmd.sunk | while | flops 5408944128 | bytes 264601872 | solution.py:207
  934.4 13.6 fusion.185
  994.1 13.6 fusion.185
  1053.8 13.6 fusion.185
  1102.9 20.4 all-to-all-done.7
  1126.9 44.8 %convolution_convert_fusion = bf16[2048,11264]{1,0:T(8,128)(2,1)} fusion(bf16[768,2048]{1,0:T(8,128)(2,1)} %copy-done.22, bf16[768,5632]{1,0:T(8,128)(2,1)} %get-tuple-element.291, bf16[768,5632]{1,0:T(8,128)(2,1)} %get-tuple-element.290), kind=kOutput, calls=%fused_computation.72 | convolution fusion | flops 35491151872 | bytes 66584576 | tf_op jit(solution)/shard_map/rc,re->ce/dot_general | solution.py:263
  1177.7 26.4 convolution_convert_fusion.1
  1204.1 12.2 convolution_convert_fusion.3
  1216.2 12.3 copy.197
  1305.8 10.9 fusion.117
  1327.2 13.4 convolution_convert_fusion.2
  1340.6 59.3 %pad_maximum_fusion = bf16[2048,22016]{1,0:T(8,128)(2,1)} fusion(bf16[2048,5632]{1,0:T(8,128)(2,1)} %convolution_convert_fusion.1, bf16[2048,11264]{1,0:T(8,128)(2,1)} %convolution_convert_fusion, bf16[2048,2048]{1,0:T(8,128)(2,1)} %copy.197, bf16[2048,3072]{1,0:T(8,128)(2,1)} %convolution_convert_fusion.2), kind=kLoop, calls=%fused_computation.71 | loop fusion | flops 360710144 | bytes 180355072 | tf_op jit(solution)/shard_map/concatenate | solution.py:257
  1400.0 490.8 %reduce-scatter.4.cloned.1.call-done = bf16[256,22016]{1,0:T(8,128)(2,1)} async-done(((bf16[2048,22016]{1,0:T(8,128)(2,1)}), bf16[256,22016]{1,0:T(8,128)(2,1)}) %reduce-scatter.4.cloned.1.call-update) | async-done | bytes 11272208
  1890.9 26.6 add_convert_fusion
  1917.5 72.8 %psum.7 = f32[2,2048]{1,0:T(2,128)S(1)} all-reduce(f32[2,2048]{1,0:T(2,128)S(1)} %pad_maximum_fusion.6), channel_id=1, replica_groups=mesh['fsdp'=8,'ulysses'=4] {'fsdp','ulysses'}, use_global_device_ids=true, to_apply=%region_13.14 | all-reduce | flops 4096 | bytes 32768 | tf_op jit(solution)/shard_map/psum | solution.py:249
  1990.9 653.2 %all-gather.29.cloned.1.call-done = bf16[1024,22016]{1,0:T(8,128)(2,1)} async-done(((bf16[256,22016]{1,0:T(8,128)(2,1)}), bf16[1024,22016]{1,0:T(8,128)(2,1)}) %all-gather.29.cloned.1.call-update) | async-done | bytes 45088784 | tf_op jit(solution)/shard_map/all_gather | solution.py:274
  2644.1 30.4 %reduce_sum.98 = bf16[256,22016]{1,0:T(8,128)(2,1)} reduce(bf16[4,256,22016]{2,1,0:T(8,128)(2,1)} %bitcast.404, bf16[]{:T(256)} %constant.71.clone.1), dimensions={0}, to_apply=%region_15.16 | reduce | flops 16908288 | bytes 56360960 | tf_op jit(solution)/shard_map/reduce_sum | solution.py:274
  (291 shorter events, 495.8 us)
Async XLA Ops:
  7.2 33.4 %all-gather.13.cloned.1.call-start = ((), (), s32[]{:S(2)}) async-start(), calls=%async_computation.9 | async-start | bytes 2359296 | tf_op jit(solution)/shard_map/all_gather | solution.py:66
  7.9 62.5 %all-gather.15.cloned.1.call-start = ((), (), s32[]{:S(2)}) async-start(), calls=%async_computation.10 | async-start | bytes 2359296 | tf_op jit(solution)/shard_map/all_gather | solution.py:65
  8.7 118.0 %all-gather.17.cloned.1.call-start = ((), (), s32[]{:S(2)}) async-start(), calls=%async_computation.11 | async-start | bytes 9437184 | tf_op jit(solution)/shard_map/all_gather | solution.py:64
  9.4 378.3 %all-gather.19.cloned.1.call-start = ((), (), s32[]{:S(2)}) async-start(), calls=%async_computation.12 | async-start | bytes 9437184 | tf_op jit(solution)/shard_map/all_gather | solution.py:67
  10.0 391.6 %all-gather.23.cloned.1.call-start = ((), (), s32[]{:S(2)}) async-start(), calls=%async_computation.14 | async-start | bytes 25952256 | tf_op jit(solution)/shard_map/all_gather | solution.py:130
  10.6 417.1 %all-gather.25.cloned.1.call-start = ((), (), s32[]{:S(2)}) async-start(), calls=%async_computation.15 | async-start | bytes 25952256 | tf_op jit(solution)/shard_map/all_gather | solution.py:140
  11.1 531.1 %all-gather.21.cloned.1.call-start = ((), (), s32[]{:S(2)}) async-start(), calls=%async_computation.13 | async-start | bytes 25952256 | tf_op jit(solution)/shard_map/all_gather | solution.py:129
  11.9 746.9 %all-gather.27.cloned.1.call-start = ((), (), s32[]{:S(2)}) async-start(), calls=%async_computation.16 | async-start | bytes 51904512 | tf_op jit(solution)/shard_map/all_gather | solution.py:157
  28.3 115.3 %copy-start.26 = (f32[8,1,256]{2,1,0:T(1,128)}, f32[8,1,256]{2,1,0:T(1,128)S(1)}, u32[]{:S(2)}) copy-start(f32[8,1,256]{2,1,0:T(1,128)S(1)} %convert_element_type.247) | copy-start | bytes 24580
  29.0 114.6 %copy-start.33 = (f32[3,256]{1,0:T(4,128)}, f32[3,256]{1,0:T(4,128)S(1)}, u32[]{:S(2)}) copy-start(f32[3,256]{1,0:T(4,128)S(1)} %add_rsqrt_fusion.1) | copy-start | bytes 9220
  48.8 90.2 %all-to-all-start = ((bf16[3,256,4,128]{3,1,0,2:T(8,128)(2,1)}), bf16[3,256,4,128]{3,1,0,2:T(8,128)(2,1)}, u32[]{:S(2)}, u32[]{:S(2)}) async-start(bf16[3,256,4,128]{3,1,0,2:T(8,128)(2,1)} %copy.167), calls=%async_computation | async-start | bytes 1572864 | tf_op jit(solution)/shard_map/all_to_all | solution.py:92
  55.5 98.4 %copy-start.12 = (f32[3,256,128]{1,2,0:T(8,128)}, f32[3,256,128]{1,2,0:T(8,128)S(1)}, u32[]{:S(2)}) copy-start(f32[3,256,128]{1,2,0:T(8,128)S(1)} %get-tuple-element.318) | copy-start | bytes 1179652
  139.1 25.2 all-to-all-start.1
  164.3 75.1 %all-to-all-start.2 = ((bf16[3,256,16,128]{1,3,0,2:T(8,128)(2,1)}), bf16[3,256,16,128]{1,3,0,2:T(8,128)(2,1)}, u32[]{:S(2)}, u32[]{:S(2)}) async-start(bf16[3,256,16,128]{1,3,0,2:T(8,128)(2,1)} %copy.173), calls=%async_computation.2 | async-start | bytes 6291456 | tf_op jit(solution)/shard_map/all_to_all | solution.py:90
  301.6 75.0 %all-to-all-start.3 = ((bf16[3,1024,4,128]{3,2,0,1:T(4,128)(2,1)}), bf16[3,1024,4,128]{3,2,0,1:T(4,128)(2,1)}, u32[]{:S(2)}, u32[]{:S(2)}) async-start(bf16[3,1024,4,128]{3,2,0,1:T(4,128)(2,1)} %get-tuple-element.103), calls=%async_computation.3 | async-start | bytes 6291456 | tf_op jit(solution)/shard_map/all_to_all | solution.py:122
  306.5 81.2 %copy-start.35 = (f32[768]{0:T(1024)}, f32[768]{0:T(1024)S(1)}, u32[]{:S(2)}) copy-start(f32[768]{0:T(1024)S(1)} %mul.276) | copy-start | bytes 9220
  315.4 82.9 %copy-start.28 = (f32[8,1,256]{2,1,0:T(1,128)}, f32[8,1,256]{2,1,0:T(1,128)S(1)}, u32[]{:S(2)}) copy-start(f32[8,1,256]{2,1,0:T(1,128)S(1)} %convert_element_type.248) | copy-start | bytes 24580
  401.5 140.7 %copy-start.22 = (bf16[768,2048]{1,0:T(8,128)(2,1)}, bf16[768,2048]{1,0:T(8,128)(2,1)S(1)}, u32[]{:S(2)}) copy-start(bf16[768,2048]{1,0:T(8,128)(2,1)S(1)} %multiply_convert_fusion.5) | copy-start | bytes 9437188
  758.8 25.2 copy-start.8
  758.8 25.2 copy-start.29
  758.8 25.2 copy-start.31
  830.7 75.7 %all-to-all-start.4 = ((bf16[3,256,16,128]{3,1,0,2:T(8,128)(2,1)}), bf16[3,256,16,128]{3,1,0,2:T(8,128)(2,1)S(1)}, u32[]{:S(2)}, u32[]{:S(2)}) async-start(bf16[3,256,16,128]{3,1,0,2:T(8,128)(2,1)} %copy.179), calls=%async_computation.4 | async-start | bytes 6291456 | tf_op jit(solution)/shard_map/all_to_all | solution.py:174
  912.6 185.5 %copy-start.34 = (f32[3,256]{1,0:T(4,128)S(1)}, f32[3,256]{1,0:T(4,128)}, u32[]{:S(2)}) copy-start(f32[3,256]{1,0:T(4,128)} %copy-done.33) | copy-start | bytes 9220
  1094.5 28.8 %all-to-all-start.7 = ((bf16[3,1024,1,128]{3,0,2,1:T(4,128)(2,1)}), bf16[3,1024,1,128]{3,0,2,1:T(4,128)(2,1)S(1)}, u32[]{:S(2)}, u32[]{:S(2)}) async-start(bf16[3,1024,1,128]{3,0,2,1:T(4,128)(2,1)} %copy.194), calls=%async_computation.7 | async-start | bytes 2097152 | tf_op jit(solution)/shard_map/all_to_all | solution.py:213
  1123.3 48.4 %copy-start.19 = (bf16[3,1024,1,128]{3,0,2,1:T(4,128)(2,1)}, bf16[3,1024,1,128]{3,0,2,1:T(4,128)(2,1)S(1)}, u32[]{:S(2)}) copy-start(bf16[3,1024,1,128]{3,0,2,1:T(4,128)(2,1)S(1)} %all-to-all-done.7) | copy-start | bytes 2359300
  1123.3 48.4 %all-to-all-start.6 = ((bf16[3,1024,1,128]{3,0,2,1:T(4,128)(2,1)}), bf16[3,1024,1,128]{3,0,2,1:T(4,128)(2,1)S(1)}, u32[]{:S(2)}, u32[]{:S(2)}) async-start(bf16[3,1024,1,128]{3,0,2,1:T(4,128)(2,1)} %copy.188), calls=%async_computation.6 | async-start | bytes 2097152 | tf_op jit(solution)/shard_map/all_to_all | solution.py:212
  1172.7 82.8 %all-to-all-start.5 = ((bf16[3,1024,4,128]{3,2,0,1:T(4,128)(2,1)}), bf16[3,1024,4,128]{3,2,0,1:T(4,128)(2,1)S(1)}, u32[]{:S(2)}, u32[]{:S(2)}) async-start(bf16[3,1024,4,128]{3,2,0,1:T(4,128)(2,1)} %get-tuple-element.105), calls=%async_computation.5 | async-start | bytes 6291456 | tf_op jit(solution)/shard_map/all_to_all | solution.py:211
  1177.7 713.1 %reduce-scatter.4.cloned.1.call-start = ((), (), s32[]{:S(2)}) async-start(), calls=%async_computation.18 | async-start | bytes 101449728
  1177.7 26.4 copy-start.37
  1400.0 490.8 %copy-start.38 = (f32[768]{0:T(1024)S(1)}, f32[768]{0:T(1024)}, u32[]{:S(2)}) copy-start(f32[768]{0:T(1024)} %copy-done.35) | copy-start | bytes 9220
  1400.0 1244.1 %all-gather.29.cloned.1.call-start = ((), (), s32[]{:S(2)}) async-start(), calls=%async_computation.17 | async-start | bytes 56360960 | tf_op jit(solution)/shard_map/all_gather | solution.py:274
  1890.8 26.7 copy-start.39
  (43 other events, 356.8 us)
Sparse Core Ops, SparseCore 0:
  9.9 30.6 all-gather.12
  42.4 27.8 all-gather.14
  72.3 54.3 all-gather.16
  128.4 54.3 all-gather.18
  184.6 116.4 all-gather.22
  302.8 120.9 all-gather.24
  425.7 116.4 all-gather.20
  544.7 214.1 all-gather.26
  1400.1 490.6 reduce-scatter.3
  1892.2 751.8 all-gather.28
